TPU v7x, 256 devices: a whole 4x4x8 slice. The times are simulated.
256 devices in a mesh: seq: 32 (over x, y, core), head: 8 (over z).
Axes of the slice: x: 4, y: 4, z: 8, core: 2. Of those that a mesh axis runs over, the one named last changes fastest.
Arguments:
- queries: bfloat16 [32768, 64, 128], P(('seq', 'head')), may hold values from -8 to 8
- keys: bfloat16 [32768, 8, 128], P(('seq', 'head')), may hold values from -8 to 8
- values: bfloat16 [32768, 8, 128], P(('seq', 'head')), may hold values from -6 to 6
- ancestors: int32 [256, 8], P('seq'), may hold values from 0 to 255, as said below
- lengths: int32 [256], replicated, may hold values from 2 to 128
Outputs:
- attended: bfloat16 [32768, 64, 128], P(('seq', 'head'))
Inputs may be any that keep to these rules, and one draw needn't show every extreme that they name: The 8 ancestors of a block are distinct blocks held on other indices of seq; the blocks of one index of seq name, all together, exactly 2 distinct blocks of each of 6 other indices and no other block.
All inputs are finite; a program needn't handle non-finite values.
Results may differ from a plain program's by a relative error of at most 0.0049.
Values may be sent and summed in bfloat16 or wider, within the bound.
No kernel may reach another device: no remote copies, remote signals or barrier semaphores. Data moves between devices by JAX's collectives and lax.ppermute only.
A program may use at most 64 MiB of HBM per device.

v0:
```python
import math
import jax
import jax.numpy as jnp
from jax import lax
from jax.sharding import PartitionSpec as P

BS = 128
negative_fill = -1e30


def attend_block(query_block, key_self, value_self, key_far, value_far, length_self, length_far):
    width = query_block.shape[-1]
    block_rows = key_self.shape[0]
    kv_groups = key_self.shape[1]
    far_count = key_far.shape[0]
    key_all = jnp.concatenate([key_self[None], key_far], axis=0).reshape(-1, kv_groups, width)
    value_all = jnp.concatenate([value_self[None], value_far], axis=0).reshape(-1, kv_groups, width)
    scores = jnp.einsum("tgsd,kgd->gstk", query_block, key_all, preferred_element_type=jnp.float32)
    scores = scores * (1.0 / math.sqrt(width))
    offsets_row = jnp.arange(block_rows, dtype=jnp.int32)
    self_mask = (offsets_row[None, :] <= offsets_row[:, None]) & (
        offsets_row[None, :] < length_self
    )
    far_mask = (offsets_row[None, :] < length_far[:, None]).reshape(1, far_count * block_rows)
    far_mask = jnp.broadcast_to(far_mask, (block_rows, far_count * block_rows))
    allowed = jnp.concatenate([self_mask, far_mask], axis=1)
    scores = jnp.where(allowed, scores, negative_fill)
    largest = jnp.max(scores, axis=-1, keepdims=True)
    exponent = jnp.exp(scores - largest)
    weights = (exponent / jnp.sum(exponent, axis=-1, keepdims=True)).astype(jnp.bfloat16)
    mixed = jnp.einsum("gstk,kgd->tgsd", weights, value_all, preferred_element_type=jnp.float32)
    return mixed.astype(jnp.bfloat16)


def attend_items(items):
    query_block, key_self, value_self, key_far, value_far, length_self, length_far = items
    return attend_block(
        query_block, key_self, value_self, key_far, value_far, length_self, length_far
    )


def local(queries, keys, values, ancestors, lengths):
    query_local, key_local, value_local = (
        lax.all_to_all(queries, "head", split_axis=1, concat_axis=0, tiled=True),
        lax.all_to_all(keys, "head", split_axis=1, concat_axis=0, tiled=True),
        lax.all_to_all(values, "head", split_axis=1, concat_axis=0, tiled=True),
    )
    token_rows, head_count, width = query_local.shape
    kv_groups = key_local.shape[1]
    blk_dev = token_rows // BS
    seq_place = lax.axis_index("seq")
    key_blocks = key_local.reshape(blk_dev, BS, kv_groups, width)
    value_blocks = value_local.reshape(blk_dev, BS, kv_groups, width)
    key_every, value_every = (
        lax.all_gather(key_local, "seq", axis=0, tiled=True),
        lax.all_gather(value_local, "seq", axis=0, tiled=True),
    )
    key_every = key_every.reshape(-1, BS, kv_groups, width)
    value_every = value_every.reshape(-1, BS, kv_groups, width)
    key_far = jnp.take(key_every, ancestors, axis=0)
    value_far = jnp.take(value_every, ancestors, axis=0)
    length_self = lax.dynamic_slice_in_dim(lengths, seq_place * blk_dev, blk_dev)
    length_far = jnp.take(lengths, ancestors, axis=0)
    query_blocks = query_local.reshape(blk_dev, BS, kv_groups, head_count // kv_groups, width)
    mixed = lax.map(
        attend_items,
        (query_blocks, key_blocks, value_blocks, key_far, value_far, length_self, length_far),
    )
    mixed = mixed.reshape(token_rows, head_count, width)
    return lax.all_to_all(mixed, "head", split_axis=0, concat_axis=1, tiled=True)


def solution(mesh):
    placed = (
        P(("seq", "head"), None, None),
        P(("seq", "head"), None, None),
        P(("seq", "head"), None, None),
        P("seq", None),
        P(),
    )
    return jax.shard_map(
        local, mesh=mesh, in_specs=placed, out_specs=P(("seq", "head"), None, None), check_vma=False
    )
```

profile of v0, /device:TPU:1, one launch (start us, length us, event | category | flops | bytes accessed | tf_op | source)
XLA Modules:
  0.0 284.1 jit_solution(3996163437452136307)
XLA Ops:
  6.5 1.1 copy.28
  7.7 19.4 %all_to_all.69 = bf16[128,8,128]{2,0,1:T(8,128)(2,1)} all-to-all(bf16[128,8,128]{2,0,1:T(8,128)(2,1)S(1)} %copy.28), channel_id=1, replica_groups=mesh['seq'=32,'head'=8] {'head'}, dimensions={1} | all-to-all | bytes 524288 | tf_op jit(solution)/shard_map/all_to_all | solution.py:45
  27.2 1.0 copy.27
  28.1 12.5 %all_to_all.70 = bf16[128,8,128]{2,0,1:T(8,128)(2,1)} all-to-all(bf16[128,8,128]{2,0,1:T(8,128)(2,1)S(1)} %copy.27), channel_id=1, replica_groups=mesh['seq'=32,'head'=8] {'head'}, dimensions={1} | all-to-all | bytes 524288 | tf_op jit(solution)/shard_map/all_to_all | solution.py:46
  40.7 2.7 copy.29
  43.4 4.5 %all-to-all-start.2 = ((bf16[128,64,128]{2,0,1:T(8,128)(2,1)}), bf16[128,64,128]{2,0,1:T(8,128)(2,1)}, u32[]{:S(2)}, u32[]{:S(2)}) async-start(bf16[128,64,128]{2,0,1:T(8,128)(2,1)} %copy.29), calls=%async_computation.2 | async-start | bytes 4194304 | tf_op jit(solution)/shard_map/all_to_all | solution.py:44
  48.1 0.8 gather_fusion
  48.9 34.5 %all-gather.5.cloned.1.call-done = bf16[32768,1,128]{2,0,1:T(8,128)(2,1)} async-done(((bf16[1024,1,128]{2,0,1:T(8,128)(2,1)}), bf16[32768,1,128]{2,0,1:T(8,128)(2,1)}) %all-gather.5.cloned.1.call-update) | async-done | bytes 8388624 | tf_op jit(solution)/shard_map/all_gather | solution.py:55
  83.5 4.3 %gather_fusion.2 = bf16[64,128,128]{2,1,0:T(8,128)(2,1)S(1)} fusion(bf16[256,128,128]{2,1,0:T(8,128)(2,1)} %bitcast.124, s32[1024]{0:T(1024)S(1)} %pad_clamp_fusion), kind=kCustom, calls=%fused_computation.1.clone | custom fusion | bytes 4194560 | tf_op jit(solution)/shard_map/jit(_take)/gather | solution.py:60
  87.8 55.7 %all-gather.3.cloned.1.call-done = bf16[32768,1,128]{2,0,1:T(8,128)(2,1)} async-done(((bf16[1024,1,128]{2,0,1:T(8,128)(2,1)}), bf16[32768,1,128]{2,0,1:T(8,128)(2,1)}) %all-gather.3.cloned.1.call-update) | async-done | bytes 8388624 | tf_op jit(solution)/shard_map/all_gather | solution.py:56
  143.5 5.6 %gather_fusion.1 = bf16[64,128,128]{2,1,0:T(8,128)(2,1)} fusion(bf16[256,128,128]{2,1,0:T(8,128)(2,1)} %bitcast.125, s32[1024]{0:T(1024)S(1)} %pad_clamp_fusion), kind=kCustom, calls=%fused_computation.clone | custom fusion | bytes 4194560 | tf_op jit(solution)/shard_map/jit(_take)/gather | solution.py:61
  149.1 1.6 broadcast_select_fusion
  151.7 65.8 %while.10 = (s32[]{:T(128)}, bf16[8,128,1,8,128]{4,3,1,0,2:T(8,128)(2,1)}, bf16[8,128,1,128]{3,1,0,2:T(8,128)(2,1)}, bf16[8,8,128,1,128]{4,2,1,3,0:T(8,128)(2,1)...) while((s32[]{:T(128)}, ...), condition=%wide.region_3.5_spmd, body=%wide.region_0.4_spmd.sunk | while | flops 616381568 | bytes 19325688 | solution.py:65
  153.1 0.8 constant_dynamic-slice_fusion.4
  154.1 1.0 dynamic-slice_bitcast_fusion.3
  155.1 1.8 fusion.34
  156.9 0.8 fusion.35
  157.8 1.3 fusion.36
  162.3 1.0 dynamic-slice_bitcast_fusion.3
  163.4 1.8 fusion.34
  165.2 0.8 fusion.35
  166.0 1.3 fusion.36
  170.5 1.0 dynamic-slice_bitcast_fusion.3
  171.6 1.8 fusion.34
  173.4 0.8 fusion.35
  174.2 1.3 fusion.36
  178.8 1.0 dynamic-slice_bitcast_fusion.3
  179.8 1.8 fusion.34
  181.6 0.8 fusion.35
  182.4 1.3 fusion.36
  187.0 1.0 dynamic-slice_bitcast_fusion.3
  188.1 1.8 fusion.34
  189.8 0.8 fusion.35
  190.7 1.3 fusion.36
  195.2 1.0 dynamic-slice_bitcast_fusion.3
  196.3 1.8 fusion.34
  198.1 0.8 fusion.35
  198.9 1.3 fusion.36
  203.4 1.0 dynamic-slice_bitcast_fusion.3
  204.5 1.8 fusion.34
  206.3 0.8 fusion.35
  207.1 1.3 fusion.36
  211.7 1.0 dynamic-slice_bitcast_fusion.3
  212.7 1.8 fusion.34
  214.5 0.8 fusion.35
  215.3 1.3 fusion.36
  217.5 57.8 %all_to_all.71 = bf16[1024,8,128]{2,1,0:T(8,128)(2,1)S(1)} all-to-all(bf16[1024,8,128]{2,1,0:T(8,128)(2,1)} %bitcast.119), channel_id=1, replica_groups=mesh['seq'=32,'head'=8] {'head'}, dimensions={0} | all-to-all | bytes 4194304 | tf_op jit(solution)/shard_map/all_to_all | solution.py:70
  275.3 1.9 copy.39
  (116 shorter events, 27.1 us)
Async XLA Ops:
  6.5 34.1 %copy-start.2 = (bf16[128,64,128]{2,1,0:T(8,128)(2,1)S(1)}, bf16[128,64,128]{2,1,0:T(8,128)(2,1)}, u32[]{:S(2)}) copy-start(bf16[128,64,128]{2,1,0:T(8,128)(2,1)} %param.9) | copy-start | bytes 6291460
  6.5 76.9 %all-gather.5.cloned.1.call-start = ((), (), s32[]{:S(2)}) async-start(), calls=%async_computation.5 | async-start | bytes 8650752 | tf_op jit(solution)/shard_map/all_gather | solution.py:55
  27.1 116.4 %all-gather.3.cloned.1.call-start = ((), (), s32[]{:S(2)}) async-start(), calls=%async_computation.4 | async-start | bytes 8650752 | tf_op jit(solution)/shard_map/all_gather | solution.py:56
  43.4 4.5 %copy-start.3 = (s32[8,8]{1,0:T(8,128)S(1)}, s32[8,8]{1,0:T(8,128)}, u32[]{:S(2)}) copy-start(s32[8,8]{1,0:T(8,128)} %param.12) | copy-start | bytes 772
  43.4 4.6 %copy-start = (s32[256]{0:T(256)S(1)}, s32[256]{0:T(256)}, u32[]{:S(2)}) copy-start(s32[256]{0:T(256)} %param.13) | copy-start | bytes 3076
  43.4 108.3 %all-to-all-start.2 = ((bf16[128,64,128]{2,0,1:T(8,128)(2,1)}), bf16[128,64,128]{2,0,1:T(8,128)(2,1)}, u32[]{:S(2)}, u32[]{:S(2)}) async-start(bf16[128,64,128]{2,0,1:T(8,128)(2,1)} %copy.29), calls=%async_computation.2 | async-start | bytes 4194304 | tf_op jit(solution)/shard_map/all_to_all | solution.py:44
  149.1 2.3 copy-start.1
Sparse Core Ops, SparseCore 0:
  27.2 56.1 all-gather.4
  86.0 57.4 all-gather.2
where the time goes:
time: 286 us; the launch traced here: 284 us
  waiting for transfers between devices  90.2 us (32%)
  blocking collectives  89.7 us (31%)
  local copies, waits for them, and re-layouts  44.8 us (16%)
  matrix products  24.2 us (8%)
  other arithmetic  16.5 us (6%)
  between operations  13.5 us (5%)
  starting transfers between devices  4.53 us (2%)
    all_to_all x1, blocking collectives, local(): lax.all_to_all(mixed, 'head', split_axis=0, concat_axis=1, tiled=True)  57.8 us
    all_gather x1, waiting for transfers between devices, local(): lax.all_gather(value_local, 'seq', axis=0, tiled=True)  55.7 us
    all_gather x1, waiting for transfers between devices, local(): lax.all_gather(key_local, 'seq', axis=0, tiled=True)  34.5 us
    all_to_all x1, blocking collectives, local(): lax.all_to_all(keys, 'head', split_axis=1, concat_axis=0, tiled=True)  19.4 us
    dot_general x8, matrix products, attend_block(): jnp.einsum('tgsd,kgd->gstk', query_block, key_all, preferred_element_type...  14.2 us
    all_to_all x1, blocking collectives, local(): lax.all_to_all(values, 'head', split_axis=1, concat_axis=0, tiled=True)  12.5 us
    dynamic_slice x16, local copies, waits for them, and re-layouts, local(): lax.map(attend_items, (query_blocks, key_blocks, value_blocks, key_far, v...  11 us
    dot_general x8, matrix products, attend_block(): jnp.einsum('gstk,kgd->tgsd', weights, value_all, preferred_element_type=j...  10 us
  transfers between devices with their start and end apart: 3, of which 2 were waited for; matrix products, arithmetic and copies ran while one was open for 6% of the time, Pallas kernels for 0%

commit v1 on v0

--- a/solution.py
+++ b/solution.py
@@ -42,7 +42,12 @@
 def local(queries, keys, values, ancestors, lengths):
     query_local, key_local, value_local = (
         lax.all_to_all(queries, "head", split_axis=1, concat_axis=0, tiled=True),
-        lax.all_to_all(keys, "head", split_axis=1, concat_axis=0, tiled=True),
+        jnp.concatenate(
+            lax.all_to_all(
+                jnp.stack(jnp.split(keys, lax.axis_size("head"), axis=1), axis=0), "head", 0, 0
+            ),
+            axis=0,
+        ),
         lax.all_to_all(values, "head", split_axis=1, concat_axis=0, tiled=True),
     )
     token_rows, head_count, width = query_local.shape

time: 286 us -> 287 us (level)
    all_gather x1, waiting for transfers between devices: 55.7 us -> 32.7 us  [local(): lax.all_gather(value_local, 'seq', axis=0, tiled=True)]
    all_gather x1, waiting for transfers between devices: 34.5 us -> 55.7 us  [local(): lax.all_gather(key_local, 'seq', axis=0, tiled=True)]
    all_to_all x1, blocking collectives: 12.5 us -> 19.4 us  [local(): lax.all_to_all(values, 'head', split_axis=1, concat_axis=0, tiled=True)]
    all_to_all x1, blocking collectives: 19.4 us -> 12.5 us  [local(): lax.all_to_all(jnp.stack(jnp.split(keys, lax.axis_size('head'), axis=1),...]
where the time goes in v1:
time: 287 us; the launch traced here: 285 us
  blocking collectives  89.7 us (31%)
  waiting for transfers between devices  88.4 us (31%)
  local copies, waits for them, and re-layouts  47 us (16%)
  matrix products  24.2 us (8%)
  other arithmetic  17.2 us (6%)
  between operations  13.5 us (5%)
  starting transfers between devices  4.54 us (2%)
    all_to_all x1, blocking collectives, local(): lax.all_to_all(mixed, 'head', split_axis=0, concat_axis=1, tiled=True)  57.8 us
    all_gather x1, waiting for transfers between devices, local(): lax.all_gather(key_local, 'seq', axis=0, tiled=True)  55.7 us
    all_gather x1, waiting for transfers between devices, local(): lax.all_gather(value_local, 'seq', axis=0, tiled=True)  32.7 us
    all_to_all x1, blocking collectives, local(): lax.all_to_all(values, 'head', split_axis=1, concat_axis=0, tiled=True)  19.4 us
    dot_general x8, matrix products, attend_block(): jnp.einsum('tgsd,kgd->gstk', query_block, key_all, preferred_element_type...  14.2 us
    all_to_all x1, blocking collectives, local(): lax.all_to_all(jnp.stack(jnp.split(keys, lax.axis_size('head'), axis=1),...  12.5 us
    dynamic_slice x16, local copies, waits for them, and re-layouts, local(): lax.map(attend_items, (query_blocks, key_blocks, value_blocks, key_far, v...  11.4 us
    dot_general x8, matrix products, attend_block(): jnp.einsum('gstk,kgd->tgsd', weights, value_all, preferred_element_type=j...  10 us
  transfers between devices with their start and end apart: 3, of which 2 were waited for; matrix products, arithmetic and copies ran while one was open for 6% of the time, Pallas kernels for 0%

profile of v1, /device:TPU:1, one launch (start us, length us, event | category | flops | bytes accessed | tf_op | source)
XLA Modules:
  0.0 285.3 jit_solution(1244063264035617248)
XLA Ops:
  6.5 1.1 copy.48
  7.7 19.4 %all_to_all.56 = bf16[128,8,128]{2,0,1:T(8,128)(2,1)} all-to-all(bf16[128,8,128]{2,0,1:T(8,128)(2,1)S(1)} %copy.48), channel_id=1, replica_groups=mesh['seq'=32,'head'=8] {'head'}, dimensions={1} | all-to-all | bytes 524288 | tf_op jit(solution)/shard_map/all_to_all | solution.py:51
  27.2 2.6 fusion.25
  30.0 12.5 %all_to_all.57 = bf16[8,128,1,128]{3,1,2,0:T(8,128)(2,1)} all-to-all(bf16[8,128,1,128]{3,1,2,0:T(8,128)(2,1)S(1)} %fusion.17), channel_id=1, replica_groups=mesh['seq'=32,'head'=8] {'head'}, dimensions={0} | all-to-all | bytes 524288 | tf_op jit(solution)/shard_map/all_to_all | solution.py:46
  42.5 2.7 copy.57
  45.2 4.5 %all-to-all-start.2 = ((bf16[128,64,128]{2,0,1:T(8,128)(2,1)}), bf16[128,64,128]{2,0,1:T(8,128)(2,1)}, u32[]{:S(2)}, u32[]{:S(2)}) async-start(bf16[128,64,128]{2,0,1:T(8,128)(2,1)} %copy.57), calls=%async_computation.2 | async-start | bytes 4194304 | tf_op jit(solution)/shard_map/all_to_all | solution.py:44
  49.9 0.8 gather_fusion
  50.8 32.7 %all-gather.3.cloned.1.call-done = bf16[32768,1,128]{2,0,1:T(8,128)(2,1)} async-done(((bf16[1024,1,128]{2,0,1:T(8,128)(2,1)}), bf16[32768,1,128]{2,0,1:T(8,128)(2,1)}) %all-gather.3.cloned.1.call-update) | async-done | bytes 8388624 | tf_op jit(solution)/shard_map/all_gather | solution.py:61
  83.5 4.3 %gather_fusion.1 = bf16[64,128,128]{2,1,0:T(8,128)(2,1)S(1)} fusion(bf16[256,128,128]{2,1,0:T(8,128)(2,1)} %bitcast.153, s32[1024]{0:T(1024)S(1)} %pad_clamp_fusion), kind=kCustom, calls=%fused_computation.clone | custom fusion | bytes 4194560 | tf_op jit(solution)/shard_map/jit(_take)/gather | solution.py:66
  87.8 55.7 %all-gather.5.cloned.1.call-done = bf16[32768,1,128]{2,0,1:T(8,128)(2,1)} async-done(((bf16[1024,1,128]{2,0,1:T(8,128)(2,1)}), bf16[32768,1,128]{2,0,1:T(8,128)(2,1)}) %all-gather.5.cloned.1.call-update) | async-done | bytes 8388624 | tf_op jit(solution)/shard_map/all_gather | solution.py:60
  143.5 5.5 %gather_fusion.2 = bf16[64,128,128]{2,1,0:T(8,128)(2,1)} fusion(bf16[256,128,128]{2,1,0:T(8,128)(2,1)} %bitcast.154, s32[1024]{0:T(1024)S(1)} %pad_clamp_fusion), kind=kCustom, calls=%fused_computation.1.clone | custom fusion | bytes 4194560 | tf_op jit(solution)/shard_map/jit(_take)/gather | solution.py:65
  149.0 1.6 select_bitcast_fusion
  151.6 67.1 %while.10 = (s32[]{:T(128)}, bf16[8,128,1,8,128]{4,3,1,0,2:T(8,128)(2,1)}, bf16[8,128,1,128]{3,1,0,2:T(8,128)(2,1)}, bf16[8,8,128,1,128]{4,2,1,3,0:T(8,128)(2,1)...) while((s32[]{:T(128)}, ...), condition=%wide.region_3.5_spmd, body=%wide.region_0.4_spmd.sunk | while | flops 616381568 | bytes 19325688 | solution.py:70
  153.2 0.8 constant_dynamic-slice_fusion.4
  154.2 1.0 dynamic-slice_bitcast_fusion.3
  155.2 1.8 fusion.43
  157.0 0.8 fusion.44
  157.8 1.3 fusion.45
  162.6 1.0 dynamic-slice_bitcast_fusion.3
  163.6 1.8 fusion.43
  165.4 0.8 fusion.44
  166.2 1.2 fusion.45
  170.9 1.0 dynamic-slice_bitcast_fusion.3
  172.0 1.8 fusion.43
  173.8 0.8 fusion.44
  174.6 1.3 fusion.45
  179.3 1.0 dynamic-slice_bitcast_fusion.3
  180.4 1.8 fusion.43
  182.2 0.8 fusion.44
  183.0 1.2 fusion.45
  187.7 1.0 dynamic-slice_bitcast_fusion.3
  188.8 1.8 fusion.43
  190.6 0.8 fusion.44
  191.4 1.3 fusion.45
  196.1 1.0 dynamic-slice_bitcast_fusion.3
  197.2 1.8 fusion.43
  198.9 0.8 fusion.44
  199.8 1.2 fusion.45
  204.5 1.0 dynamic-slice_bitcast_fusion.3
  205.5 1.8 fusion.43
  207.3 0.8 fusion.44
  208.1 1.3 fusion.45
  212.9 1.0 dynamic-slice_bitcast_fusion.3
  213.9 1.8 fusion.43
  215.7 0.8 fusion.44
  216.5 1.2 fusion.45
  218.7 57.8 %all_to_all.58 = bf16[1024,8,128]{2,1,0:T(8,128)(2,1)S(1)} all-to-all(bf16[1024,8,128]{2,1,0:T(8,128)(2,1)} %bitcast.148), channel_id=1, replica_groups=mesh['seq'=32,'head'=8] {'head'}, dimensions={0} | all-to-all | bytes 4194304 | tf_op jit(solution)/shard_map/all_to_all | solution.py:75
  276.5 1.9 copy.100
  (124 shorter events, 28.5 us)
Async XLA Ops:
  6.5 36.0 %copy-start.2 = (bf16[128,64,128]{2,1,0:T(8,128)(2,1)S(1)}, bf16[128,64,128]{2,1,0:T(8,128)(2,1)}, u32[]{:S(2)}) copy-start(bf16[128,64,128]{2,1,0:T(8,128)(2,1)} %param.9) | copy-start | bytes 6291460
  6.5 76.9 %all-gather.3.cloned.1.call-start = ((), (), s32[]{:S(2)}) async-start(), calls=%async_computation.4 | async-start | bytes 8650752 | tf_op jit(solution)/shard_map/all_gather | solution.py:61
  27.1 116.4 %all-gather.5.cloned.1.call-start = ((), (), s32[]{:S(2)}) async-start(), calls=%async_computation.5 | async-start | bytes 8650752 | tf_op jit(solution)/shard_map/all_gather | solution.py:60
  45.2 4.5 %copy-start.3 = (s32[8,8]{1,0:T(8,128)S(1)}, s32[8,8]{1,0:T(8,128)}, u32[]{:S(2)}) copy-start(s32[8,8]{1,0:T(8,128)} %param.12) | copy-start | bytes 772
  45.2 4.6 %copy-start = (s32[256]{0:T(256)S(1)}, s32[256]{0:T(256)}, u32[]{:S(2)}) copy-start(s32[256]{0:T(256)} %param.13) | copy-start | bytes 3076
  45.2 106.4 %all-to-all-start.2 = ((bf16[128,64,128]{2,0,1:T(8,128)(2,1)}), bf16[128,64,128]{2,0,1:T(8,128)(2,1)}, u32[]{:S(2)}, u32[]{:S(2)}) async-start(bf16[128,64,128]{2,0,1:T(8,128)(2,1)} %copy.57), calls=%async_computation.2 | async-start | bytes 4194304 | tf_op jit(solution)/shard_map/all_to_all | solution.py:44
  149.0 2.3 copy-start.1
Sparse Core Ops, SparseCore 0:
  27.2 56.1 all-gather.2
  86.0 57.4 all-gather.4
